TPU v7x, 512 devices: a whole 4x8x8 slice. The times are simulated.
512 devices in a mesh: pipe: 8 (over y_hi, core), ctx: 16 (over z, y_lo), dp: 4 (over x).
Axes of the slice: x: 4, y: 8 (y_hi: 4, y_lo: 2; y = y_hi * 2 + y_lo), z: 8, core: 2. Of those that a mesh axis runs over, the one named last changes fastest.
Arguments:
- state: bfloat16 [8, 4, 2048, 1024], P('pipe', 'dp', 'ctx'), may hold values from -36 to 36
- weights: bfloat16 [2, 8, 1024, 256], P(None, 'pipe'), may hold values from -0.1875 to 0.1875
- out_grad: bfloat16 [2, 8, 4, 2048, 1024], P(None, 'pipe', 'dp', 'ctx'), may hold values from -0.59765625 to 0.59765625
- start_span: int32 [8, 4], P(None, 'dp'), may hold values from 0 to 1
- block_order: int32 [32], replicated, may hold values from 0 to 31, each once
Outputs:
- state_out: bfloat16 [8, 4, 2048, 1024], P('pipe', 'dp', 'ctx')
- weight_grads: float32 [2, 8, 1024, 256], P(None, 'pipe')
All inputs are finite; a program needn't handle non-finite values.
Results may differ from a plain program's by a relative error of at most 0.012.
Values may be sent and summed in bfloat16 or wider, within the bound.
No kernel may reach another device: no remote copies, remote signals or barrier semaphores. Data moves between devices by JAX's collectives and lax.ppermute only.
A program may use at most 64 MiB of HBM per device.

v0:
```python
import math
import jax
import jax.numpy as jnp
from jax import lax
from jax.sharding import PartitionSpec as P

EPS = 1e-05


def from_behind(block, axis, distance):
    devices = range(lax.axis_size(axis))
    route = [((i - distance) % len(devices), i) for i in devices]
    return lax.ppermute(block, axis, route)


def rms_scale(values):
    return lax.rsqrt(jnp.mean(values * values, axis=-1, keepdims=True) + EPS)


def token_positions(block_order, seq_total):
    half_count = block_order.shape[0]
    half_len = seq_total // half_count
    row_ids = jnp.arange(seq_total, dtype=jnp.int32)
    selected = (row_ids // half_len)[:, None] == jnp.arange(half_count, dtype=jnp.int32)[None, :]
    block_ids = jnp.sum(jnp.where(selected, block_order[None, :], 0), axis=1)
    return block_ids * half_len + row_ids % half_len


def shards(state, weights, out_grad, start_span, block_order):
    tok_rows = state.shape[2]
    feat_width = state.shape[3]
    head_dim = weights.shape[3] // 2
    head_count = feat_width // head_dim
    group_size = math.gcd(head_count, 4)
    group_count = head_count // group_size
    span_count = weights.shape[0]
    section_count = lax.axis_size("pipe")
    seq_total = tok_rows * lax.axis_size("ctx")
    score_scale = 1.0 / math.sqrt(head_dim)
    all_positions = token_positions(block_order, seq_total)
    own_positions = lax.dynamic_slice_in_dim(
        all_positions, lax.axis_index("ctx") * tok_rows, tok_rows
    )
    causal = all_positions[None, :] <= own_positions[:, None]
    section_index = lax.axis_index("pipe")
    carried = state[0, 0]
    start_column = start_span[:, 0]
    weight_grads = jnp.zeros((span_count, feat_width, 2 * head_dim), jnp.float32)
    for tick_index in range(out_grad.shape[0]):
        anchor = (section_index - tick_index) % section_count
        first_span = jnp.sum(
            jnp.where(jnp.arange(section_count, dtype=jnp.int32) == anchor, start_column, 0)
        )
        span_index = (first_span + (anchor + tick_index) // section_count) % 2
        weight = lax.dynamic_index_in_dim(weights[:, 0], span_index, 0, keepdims=False)
        widened = carried.astype(jnp.float32)
        normed = (widened * rms_scale(widened)).astype(jnp.bfloat16)
        split_heads = widened.reshape(tok_rows, head_count, head_dim)
        queries = (split_heads * rms_scale(split_heads)).astype(jnp.bfloat16)
        projected = jnp.dot(normed, weight, preferred_element_type=jnp.float32)
        key_raw = projected[:, :head_dim]
        key_scale = rms_scale(key_raw)
        key_unit = key_raw * key_scale
        own_rows = jnp.concatenate([key_unit, projected[:, head_dim:]], axis=1).astype(jnp.bfloat16)
        gathered = lax.all_gather(own_rows, "ctx", axis=0, tiled=True)
        key_rows = gathered[:, :head_dim]
        value_rows = gathered[:, head_dim:]
        query_groups = queries.reshape(tok_rows, group_count, group_size, head_dim).transpose(
            1, 0, 2, 3
        )

        def forward_group(query_part):
            scores = (
                jnp.einsum("qhd,kd->hqk", query_part, key_rows, preferred_element_type=jnp.float32)
                * score_scale
            )
            exponent = jnp.where(causal[None], jnp.exp(scores), 0.0)
            total_weight = jnp.sum(exponent, axis=-1, keepdims=True)
            probs = (exponent / total_weight).astype(jnp.bfloat16)
            attended = jnp.einsum(
                "hqk,kd->qhd", probs, value_rows, preferred_element_type=jnp.float32
            )
            return (probs, attended)

        probs, attended = lax.map(forward_group, query_groups)
        output = attended.transpose(1, 0, 2, 3).reshape(tok_rows, feat_width)
        updated = (widened + output * rms_scale(output)).astype(jnp.bfloat16)
        carried = from_behind(updated, "pipe", 1)
        upstream = out_grad[tick_index, 0, 0]
        upstream_groups = upstream.reshape(tok_rows, group_count, group_size, head_dim).transpose(
            1, 0, 2, 3
        )
        row_delta = jnp.sum(upstream_groups.astype(jnp.float32) * attended, axis=-1).transpose(
            0, 2, 1
        )
        key_grad = jnp.zeros((tok_rows * lax.axis_size("ctx"), head_dim), jnp.float32)
        value_grad = jnp.zeros((tok_rows * lax.axis_size("ctx"), head_dim), jnp.float32)
        for head_block in range(group_count):
            prob_part = probs[head_block]
            value_grad = value_grad + jnp.einsum(
                "hqk,qhd->kd",
                prob_part,
                upstream_groups[head_block],
                preferred_element_type=jnp.float32,
            )
            prob_grad = jnp.einsum(
                "qhd,kd->hqk",
                upstream_groups[head_block],
                value_rows,
                preferred_element_type=jnp.float32,
            )
            score_grad = (
                prob_part.astype(jnp.float32)
                * (prob_grad - row_delta[head_block][..., None])
                * score_scale
            ).astype(jnp.bfloat16)
            key_grad = key_grad + jnp.einsum(
                "hqk,qhd->kd",
                score_grad,
                query_groups[head_block],
                preferred_element_type=jnp.float32,
            )
        key_sums = lax.psum_scatter(
            jnp.concatenate([key_grad, value_grad], axis=1).astype(jnp.bfloat16),
            "ctx",
            scatter_dimension=0,
            tiled=True,
        ).astype(jnp.float32)
        key_delta = key_sums[:, :head_dim]
        key_back = key_scale * (
            key_delta - key_unit * jnp.mean(key_delta * key_unit, axis=-1, keepdims=True)
        )
        grad_rows = jnp.concatenate([key_back, key_sums[:, head_dim:]], axis=1).astype(jnp.bfloat16)
        local_grad = lax.dot_general(
            normed, grad_rows, (((0,), (0,)), ((), ())), preferred_element_type=jnp.float32
        )
        span_mask = (jnp.arange(span_count, dtype=jnp.int32) == span_index).astype(jnp.float32)[
            :, None, None
        ]
        masked_grad = span_mask * local_grad
        weight_grads = weight_grads + masked_grad
    weight_grads = lax.psum(weight_grads, ("ctx", "dp"))
    return (carried[None, None], weight_grads[:, None])


def solution(mesh):
    return jax.shard_map(
        shards,
        mesh=mesh,
        in_specs=(
            P("pipe", "dp", "ctx", None),
            P(None, "pipe", None, None),
            P(None, "pipe", "dp", "ctx", None),
            P(None, "dp"),
            P(),
        ),
        out_specs=(P("pipe", "dp", "ctx", None), P(None, "pipe", None, None)),
        check_vma=False,
    )
```

profile of v0, /device:TPU:16, one launch (start us, length us, event | category | flops | bytes accessed | tf_op | source)
XLA Modules:
  0.0 990.2 jit_solution(8186478735265335391)
XLA Ops:
  7.3 1.4 fusion.99
  9.4 1.1 fusion.62
  10.5 1.2 fusion.58
  12.7 1.1 copy.149
  13.8 1.0 fusion.60
  16.2 74.4 %all-gather.3.cloned.1.call-done = bf16[2048,256]{1,0:T(8,128)(2,1)} async-done(((bf16[128,256]{1,0:T(8,128)(2,1)}), bf16[2048,256]{1,0:T(8,128)(2,1)}) %all-gather.3.cloned.1.call-update) | async-done | bytes 1048592 | tf_op jit(solution)/shard_map/all_gather | solution.py:65
  90.6 1.3 fusion.117
  91.9 0.9 broadcast.233.clone
  92.7 2.5 broadcast.232.clone2
  95.2 22.0 %while.26 = (s32[]{:T(128)}, bf16[2,4,128,2048]{2,3,1,0:T(8,128)(2,1)}, f32[2,128,4,128]{3,1,2,0:T(8,128)}, bf16[2,128,4,128]{1,3,2,0:T(8,128)(2,1)}, bf16[2048,...) while((s32[]{:T(128)}, ...), condition=%wide.region_7.8_spmd.clone, body=%wide.region_5.7_spmd.clone.sunk | while | flops 548666880 | bytes 33962720 | solution.py:85
  95.4 2.3 bitcast_reduce_fusion.4
  97.8 1.8 fusion.136
  99.6 0.9 fusion.135
  100.5 2.5 copy.225
  103.0 3.2 constant_dynamic-update-slice_fusion.4
  106.4 2.3 bitcast_reduce_fusion.4
  108.8 1.8 fusion.136
  110.6 0.9 fusion.135
  111.5 2.5 copy.225
  114.0 3.1 constant_dynamic-update-slice_fusion.4
  117.2 1.2 multiply_reduce_fusion.3
  118.4 1.4 copy.152
  120.1 1.9 collective-permute-start
  122.8 6.8 collective-permute-done
  131.7 0.9 copy.173
  132.6 1.3 multiply_reduce_fusion.1
  134.4 2.3 convolution_bitcast_fusion.6
  136.7 2.3 fusion.38
  139.0 4.0 convolution_bitcast_fusion.8
  143.1 3.4 fusion.39
  146.4 1.1 pad_maximum_fusion
  149.1 56.5 %all-gather.5.cloned.1.call-done = bf16[2048,256]{1,0:T(8,128)(2,1)} async-done(((bf16[128,256]{1,0:T(8,128)(2,1)}), bf16[2048,256]{1,0:T(8,128)(2,1)}) %all-gather.5.cloned.1.call-update) | async-done | bytes 1048592 | tf_op jit(solution)/shard_map/all_gather | solution.py:65
  205.6 1.3 fusion.116
  207.7 2.5 broadcast.232.clone
  210.1 22.0 %while.27 = (s32[]{:T(128)}, bf16[2,4,128,2048]{2,3,1,0:T(8,128)(2,1)}, f32[2,128,4,128]{3,1,2,0:T(8,128)}, bf16[2,128,4,128]{1,3,2,0:T(8,128)(2,1)}, bf16[2048,...) while((s32[]{:T(128)}, ...), condition=%wide.region_15.16_spmd.clone, body=%wide.region_13.15_spmd.clone.sunk | while | flops 548666880 | bytes 33962720 | solution.py:85
  210.4 2.3 bitcast_reduce_fusion.5
  212.7 1.8 fusion.140
  214.6 0.9 fusion.139
  215.5 2.5 copy.226
  218.0 3.2 constant_dynamic-update-slice_fusion.5
  221.4 2.3 bitcast_reduce_fusion.5
  223.7 1.8 fusion.140
  225.6 0.9 fusion.139
  226.5 2.5 copy.226
  229.0 3.1 constant_dynamic-update-slice_fusion.5
  232.1 1.4 multiply_reduce_fusion
  233.6 2.3 convolution_bitcast_fusion.2
  235.9 2.3 fusion.36
  238.2 3.9 convolution_bitcast_fusion.4
  242.1 4.0 fusion.37
  246.2 2.2 pad_maximum_fusion.1
  248.4 35.8 %reduce-scatter.3.cloned.1.call-done = bf16[128,256]{1,0:T(8,128)(2,1)} async-done(((bf16[2048,256]{1,0:T(8,128)(2,1)}), bf16[128,256]{1,0:T(8,128)(2,1)}) %reduce-scatter.3.cloned.1.call-update) | async-done | bytes 65552 | tf_op jit(solution)/shard_map/reduce_scatter | solution.py:123
  284.9 0.9 fusion.76
  285.9 0.9 fusion.78
  287.2 73.8 %reduce-scatter.5.cloned.1.call-done = bf16[128,256]{1,0:T(8,128)(2,1)} async-done(((bf16[2048,256]{1,0:T(8,128)(2,1)}), bf16[128,256]{1,0:T(8,128)(2,1)}) %reduce-scatter.5.cloned.1.call-update) | async-done | bytes 65552 | tf_op jit(solution)/shard_map/reduce_scatter | solution.py:123
  360.9 0.9 fusion.79
  362.7 0.9 fusion.81
  363.9 1.7 add_bitcast_fusion
  365.6 1.4 copy.156
  367.2 1.2 multiply_reduce_fusion.2
  368.5 1.9 collective-permute-start.1
  370.5 7.2 collective-permute-done.1
  377.7 602.2 %all-reduce.2.cloned.1.call-done = f32[2,1,1024,256]{3,2,1,0:T(8,128)} async-done(((f32[2,1,1024,256]{3,2,1,0:T(8,128)}), f32[2,1,1024,256]{3,2,1,0:T(8,128)}) %all-reduce.2.cloned.1.call-update) | async-done | bytes 2097168 | tf_op jit(solution)/shard_map/psum | solution.py:142
  980.6 3.0 copy.256
  (128 shorter events, 12.0 us)
Async XLA Ops:
  7.2 3.3 copy-start
  7.2 8.0 copy-start.23
  7.2 83.4 %all-gather.3.cloned.1.call-start = ((), (), s32[]{:S(2)}) async-start(), calls=%async_computation.2 | async-start | bytes 1114112 | tf_op jit(solution)/shard_map/all_gather | solution.py:65
  10.5 1.4 copy-start.19
  12.6 192.9 %all-gather.5.cloned.1.call-start = ((), (), s32[]{:S(2)}) async-start(), calls=%async_computation.3 | async-start | bytes 1114112 | tf_op jit(solution)/shard_map/all_gather | solution.py:65
  95.2 24.8 %copy-start.1 = (bf16[1,1,128,1024]{3,2,1,0:T(8,128)(2,1)S(1)}, bf16[1,1,128,1024]{3,2,1,0:T(8,128)(2,1)}, u32[]{:S(2)}) copy-start(bf16[1,1,128,1024]{3,2,1,0:T(8,128)(2,1)} %param.9) | copy-start | bytes 786436
  95.2 2.6 copy-start.13
  95.2 2.6 copy-start.15
  103.0 3.2 copy-start.14
  103.0 3.2 copy-start.16
  106.2 2.6 copy-start.13
  106.2 2.6 copy-start.15
  114.0 3.1 copy-start.14
  114.0 3.1 copy-start.16
  117.1 14.0 %copy-start.8 = (bf16[2,1,1,128,1024]{4,3,2,1,0:T(8,128)(2,1)S(1)}, bf16[2,1,1,128,1024]{4,3,2,1,0:T(8,128)(2,1)}, u32[]{:S(2)}) copy-start(bf16[2,1,1,128,1024]{4,3,2,1,0:T(8,128)(2,1)} %param.11) | copy-start | bytes 1572868
  120.1 9.4 collective-permute-start
  129.6 18.6 %copy-start.2 = (bf16[128,1024]{1,0:T(8,128)(2,1)}, bf16[128,1024]{1,0:T(8,128)(2,1)S(1)}, u32[]{:S(2)}) copy-start(bf16[128,1024]{1,0:T(8,128)(2,1)S(1)} %collective-permute-done) | copy-start | bytes 786436
  129.7 0.6 copy-start.21
  130.0 4.4 copy-start.5
  130.3 0.9 copy-start.17
  131.1 153.1 %reduce-scatter.3.cloned.1.call-start = ((), (), s32[]{:S(2)}) async-start(), calls=%async_computation.4 | async-start | bytes 1114112 | tf_op jit(solution)/shard_map/reduce_scatter | solution.py:123
  147.6 213.4 %reduce-scatter.5.cloned.1.call-start = ((), (), s32[]{:S(2)}) async-start(), calls=%async_computation.5 | async-start | bytes 1114112 | tf_op jit(solution)/shard_map/reduce_scatter | solution.py:123
  210.1 2.6 copy-start.9
  210.1 2.6 copy-start.11
  218.0 3.2 copy-start.10
  218.0 3.2 copy-start.12
  221.2 2.6 copy-start.9
  221.2 2.6 copy-start.11
  229.0 3.1 copy-start.10
  229.0 3.1 copy-start.12
  232.1 3.8 copy-start.4
  232.1 6.1 copy-start.7
  242.1 44.6 %copy-start.20 = (f32[128]{0:T(128)S(1)}, f32[128]{0:T(128)}, u32[]{:S(2)}) copy-start(f32[128]{0:T(128)} %copy-done.19) | copy-start | bytes 1540
  246.1 114.8 %copy-start.6 = (f32[128,256]{1,0:T(8,128)S(1)}, f32[128,256]{1,0:T(8,128)}, u32[]{:S(2)}) copy-start(f32[128,256]{1,0:T(8,128)} %copy-done.5) | copy-start | bytes 393220
  246.1 114.8 %copy-start.18 = (f32[128]{0:T(128)S(1)}, f32[128]{0:T(128)}, u32[]{:S(2)}) copy-start(f32[128]{0:T(128)} %copy-done.17) | copy-start | bytes 1540
  246.1 117.4 %copy-start.3 = (bf16[128,1024]{1,0:T(8,128)(2,1)S(1)}, bf16[128,1024]{1,0:T(8,128)(2,1)}, u32[]{:S(2)}) copy-start(bf16[128,1024]{1,0:T(8,128)(2,1)} %copy-done.2) | copy-start | bytes 786436
  246.1 117.4 %copy-start.22 = (f32[128]{0:T(128)S(1)}, f32[128]{0:T(128)}, u32[]{:S(2)}) copy-start(f32[128]{0:T(128)} %copy-done.21) | copy-start | bytes 1540
  248.4 731.6 %all-reduce.2.cloned.1.call-start = ((), (), s32[]{:S(2)}) async-start(), calls=%async_computation.6 | async-start | bytes 4194304 | tf_op jit(solution)/shard_map/psum | solution.py:142
  368.5 9.2 collective-permute-start.1
Sparse Core Ops, SparseCore 0:
  12.8 77.7 all-gather.2
  131.2 74.3 all-gather.4
  208.4 75.7 reduce-scatter.2
  287.7 73.2 reduce-scatter.4
  365.7 614.1 all-reduce.1
where the time goes:
time: 992 us; the launch traced here: 990 us
  waiting for transfers between devices  857 us (86%)
  local copies, waits for them, and re-layouts  44.1 us (4%)
  matrix products  43.5 us (4%)
  other arithmetic  25.8 us (3%)
  between operations  15.7 us (2%)
    psum x1, waiting for transfers between devices, shards(): weight_grads = lax.psum(weight_grads, ('ctx', 'dp'))  602 us
    all_gather x2, waiting for transfers between devices, shards(): gathered = lax.all_gather(own_rows, 'ctx', axis=0, tiled=True)  131 us
    reduce_scatter x2, waiting for transfers between devices, shards(): lax.psum_scatter(jnp.concatenate([key_grad, value_grad], axis=1).astype(j...  110 us
    dynamic_update_slice x8, local copies, waits for them, and re-layouts, shards(): probs, attended = lax.map(forward_group, query_groups)  22.5 us
  transfers between devices with their start and end apart: 7, of which 7 were waited for; matrix products, arithmetic and copies ran while one was open for 7% of the time, Pallas kernels for 0%

commit v1 on v0

--- a/solution.py
+++ b/solution.py
@@ -5,6 +5,11 @@
 from jax.sharding import PartitionSpec as P
 
 EPS = 1e-05
+
+
+def _arrange_pipes(mine_x):
+    response = lax.psum(mine_x, axis_name="dp")
+    return lax.psum(response, axis_name="ctx")
 
 
 def from_behind(block, axis, distance):
@@ -139,7 +144,7 @@
         ]
         masked_grad = span_mask * local_grad
         weight_grads = weight_grads + masked_grad
-    weight_grads = lax.psum(weight_grads, ("ctx", "dp"))
+    weight_grads = _arrange_pipes(weight_grads)
     return (carried[None, None], weight_grads[:, None])
 
 

time: 992 us -> 606 us (0.61)
  the two profiles are of different devices: /device:TPU:16 before, /device:TPU:2 now
where the time goes in v1:
time: 606 us; the launch traced here: 605 us
  waiting for transfers between devices  471 us (78%)
  local copies, waits for them, and re-layouts  44.1 us (7%)
  matrix products  43.5 us (7%)
  other arithmetic  25.8 us (4%)
  between operations  16 us (3%)
    psum x1, waiting for transfers between devices, _arrange_pipes(): return lax.psum(response, axis_name='ctx')  149 us
    all_gather x2, waiting for transfers between devices, shards(): gathered = lax.all_gather(own_rows, 'ctx', axis=0, tiled=True)  130 us
    reduce_scatter x2, waiting for transfers between devices, shards(): lax.psum_scatter(jnp.concatenate([key_grad, value_grad], axis=1).astype(j...  109 us
    psum x1, waiting for transfers between devices, _arrange_pipes(): response = lax.psum(mine_x, axis_name='dp')  65.8 us
    dynamic_update_slice x8, local copies, waits for them, and re-layouts, shards(): probs, attended = lax.map(forward_group, query_groups)  22.5 us
    ppermute x2, waiting for transfers between devices, from_behind(): return lax.ppermute(block, axis, route)  16.7 us
    dot_general x4, matrix products, shards(): jnp.einsum('hqk,qhd->kd', score_grad, query_groups[head_block], preferred...  15.3 us
  transfers between devices with their start and end apart: 8, of which 8 were waited for; matrix products, arithmetic and copies ran while one was open for 11% of the time, Pallas kernels for 0%

profile of v1, /device:TPU:2, one launch (start us, length us, event | category | flops | bytes accessed | tf_op | source)
XLA Modules:
  0.0 604.6 jit_solution(1136048243943000443)
XLA Ops:
  7.3 1.4 fusion.99
  9.4 1.1 fusion.62
  10.5 1.2 fusion.58
  12.7 1.1 copy.149
  13.8 1.0 fusion.60
  16.2 74.6 %all-gather.3.cloned.1.call-done = bf16[2048,256]{1,0:T(8,128)(2,1)} async-done(((bf16[128,256]{1,0:T(8,128)(2,1)}), bf16[2048,256]{1,0:T(8,128)(2,1)}) %all-gather.3.cloned.1.call-update) | async-done | bytes 1048592 | tf_op jit(solution)/shard_map/all_gather | solution.py:70
  90.7 1.3 fusion.117
  92.9 2.5 broadcast.232.clone2
  95.3 22.0 %while.26 = (s32[]{:T(128)}, bf16[2,4,128,2048]{2,3,1,0:T(8,128)(2,1)}, f32[2,128,4,128]{3,1,2,0:T(8,128)}, bf16[2,128,4,128]{1,3,2,0:T(8,128)(2,1)}, bf16[2048,...) while((s32[]{:T(128)}, ...), condition=%wide.region_7.8_spmd.clone, body=%wide.region_5.7_spmd.clone.sunk | while | flops 548666880 | bytes 33962720 | solution.py:90
  95.6 2.3 bitcast_reduce_fusion.4
  97.9 1.8 fusion.136
  99.8 0.9 fusion.135
  100.7 2.5 copy.225
  103.2 3.2 constant_dynamic-update-slice_fusion.4
  106.6 2.3 bitcast_reduce_fusion.4
  108.9 1.8 fusion.136
  110.8 0.9 fusion.135
  111.7 2.5 copy.225
  114.2 3.1 constant_dynamic-update-slice_fusion.4
  117.3 1.2 multiply_reduce_fusion.3
  118.5 1.4 copy.152
  120.3 1.9 collective-permute-start
  123.0 7.9 %collective-permute-done = bf16[128,1024]{1,0:T(8,128)(2,1)S(1)} collective-permute-done((bf16[128,1024]{1,0:T(8,128)(2,1)S(1)}, bf16[128,1024]{1,0:T(8,128)(2,1)S(1)}, u32[]{:S(2)}, u32[]{:S(2)}) %collective-permute-start) | collective-permute-done | bytes 262176 | tf_op jit(solution)/shard_map/ppermute | solution.py:18
  133.0 0.9 copy.173
  133.9 1.3 multiply_reduce_fusion.1
  135.7 2.3 convolution_bitcast_fusion.6
  138.0 2.3 fusion.38
  140.3 4.0 convolution_bitcast_fusion.8
  144.4 3.4 fusion.39
  147.7 1.1 pad_maximum_fusion
  150.4 55.4 %all-gather.5.cloned.1.call-done = bf16[2048,256]{1,0:T(8,128)(2,1)} async-done(((bf16[128,256]{1,0:T(8,128)(2,1)}), bf16[2048,256]{1,0:T(8,128)(2,1)}) %all-gather.5.cloned.1.call-update) | async-done | bytes 1048592 | tf_op jit(solution)/shard_map/all_gather | solution.py:70
  205.7 1.3 fusion.116
  207.8 2.5 broadcast.232.clone
  210.3 22.0 %while.27 = (s32[]{:T(128)}, bf16[2,4,128,2048]{2,3,1,0:T(8,128)(2,1)}, f32[2,128,4,128]{3,1,2,0:T(8,128)}, bf16[2,128,4,128]{1,3,2,0:T(8,128)(2,1)}, bf16[2048,...) while((s32[]{:T(128)}, ...), condition=%wide.region_15.16_spmd.clone, body=%wide.region_13.15_spmd.clone.sunk | while | flops 548666880 | bytes 33962720 | solution.py:90
  210.5 2.3 bitcast_reduce_fusion.5
  212.9 1.8 fusion.140
  214.7 0.9 fusion.139
  215.6 2.5 copy.226
  218.1 3.2 constant_dynamic-update-slice_fusion.5
  221.5 2.3 bitcast_reduce_fusion.5
  223.9 1.8 fusion.140
  225.7 0.9 fusion.139
  226.6 2.5 copy.226
  229.1 3.1 constant_dynamic-update-slice_fusion.5
  232.3 1.4 multiply_reduce_fusion
  233.7 2.3 convolution_bitcast_fusion.2
  236.0 2.3 fusion.36
  238.3 3.9 convolution_bitcast_fusion.4
  242.3 4.0 fusion.37
  246.3 2.2 pad_maximum_fusion.1
  248.6 36.1 %reduce-scatter.3.cloned.1.call-done = bf16[128,256]{1,0:T(8,128)(2,1)} async-done(((bf16[2048,256]{1,0:T(8,128)(2,1)}), bf16[128,256]{1,0:T(8,128)(2,1)}) %reduce-scatter.3.cloned.1.call-update) | async-done | bytes 65552 | tf_op jit(solution)/shard_map/reduce_scatter | solution.py:128
  285.4 0.9 fusion.76
  286.3 0.9 fusion.78
  287.6 73.4 %reduce-scatter.5.cloned.1.call-done = bf16[128,256]{1,0:T(8,128)(2,1)} async-done(((bf16[2048,256]{1,0:T(8,128)(2,1)}), bf16[128,256]{1,0:T(8,128)(2,1)}) %reduce-scatter.5.cloned.1.call-update) | async-done | bytes 65552 | tf_op jit(solution)/shard_map/reduce_scatter | solution.py:128
  361.0 0.9 fusion.79
  362.7 0.9 fusion.81
  364.0 1.7 multiply_add_fusion
  365.7 65.8 %all-reduce.3.cloned.1.call-done = f32[2,1024,256]{2,1,0:T(8,128)} async-done(((f32[2,1024,256]{2,1,0:T(8,128)}), f32[2,1024,256]{2,1,0:T(8,128)}) %all-reduce.3.cloned.1.call-update) | async-done | bytes 2097168 | tf_op jit(solution)/shard_map/psum | solution.py:11
  431.6 1.4 copy.156
  433.2 1.2 multiply_reduce_fusion.2
  434.5 1.9 collective-permute-start.1
  436.4 8.8 %collective-permute-done.1 = bf16[128,1024]{1,0:T(8,128)(2,1)S(1)} collective-permute-done((bf16[128,1024]{1,0:T(8,128)(2,1)S(1)}, bf16[128,1024]{1,0:T(8,128)(2,1)S(1)}, u32[]{:S(2)}, u32[]{:S(2)}) %collective-permute-start.1) | collective-permute-done | bytes 262176 | tf_op jit(solution)/shard_map/ppermute | solution.py:18
  445.3 148.7 %all-reduce.5.cloned.1.call-done = f32[2,1,1024,256]{3,2,1,0:T(8,128)} async-done(((f32[2,1,1024,256]{3,2,1,0:T(8,128)}), f32[2,1,1024,256]{3,2,1,0:T(8,128)}) %all-reduce.5.cloned.1.call-update) | async-done | bytes 2097168 | tf_op jit(solution)/shard_map/psum | solution.py:12
  594.7 3.0 copy.257
  (131 shorter events, 12.9 us)
Async XLA Ops:
  7.2 3.3 copy-start
  7.2 8.0 %copy-start.23 = (s32[32]{0:T(128)S(1)}, s32[32]{0:T(128)}, u32[]{:S(2)}) copy-start(s32[32]{0:T(128)} %param.13) | copy-start | bytes 388
  7.2 83.6 %all-gather.3.cloned.1.call-start = ((), (), s32[]{:S(2)}) async-start(), calls=%async_computation.2 | async-start | bytes 1114112 | tf_op jit(solution)/shard_map/all_gather | solution.py:70
  10.5 1.4 copy-start.19
  12.6 193.1 %all-gather.5.cloned.1.call-start = ((), (), s32[]{:S(2)}) async-start(), calls=%async_computation.3 | async-start | bytes 1114112 | tf_op jit(solution)/shard_map/all_gather | solution.py:70
  95.3 24.8 %copy-start.1 = (bf16[1,1,128,1024]{3,2,1,0:T(8,128)(2,1)S(1)}, bf16[1,1,128,1024]{3,2,1,0:T(8,128)(2,1)}, u32[]{:S(2)}) copy-start(bf16[1,1,128,1024]{3,2,1,0:T(8,128)(2,1)} %param.9) | copy-start | bytes 786436
  95.3 2.6 copy-start.13
  95.3 2.6 copy-start.15
  103.2 3.2 copy-start.14
  103.2 3.2 copy-start.16
  106.3 2.6 copy-start.13
  106.3 2.6 copy-start.15
  114.2 3.1 copy-start.14
  114.2 3.1 copy-start.16
  117.3 15.1 %copy-start.8 = (bf16[2,1,1,128,1024]{4,3,2,1,0:T(8,128)(2,1)S(1)}, bf16[2,1,1,128,1024]{4,3,2,1,0:T(8,128)(2,1)}, u32[]{:S(2)}) copy-start(bf16[2,1,1,128,1024]{4,3,2,1,0:T(8,128)(2,1)} %param.11) | copy-start | bytes 1572868
  120.3 10.6 %collective-permute-start = (bf16[128,1024]{1,0:T(8,128)(2,1)S(1)}, bf16[128,1024]{1,0:T(8,128)(2,1)S(1)}, u32[]{:S(2)}, u32[]{:S(2)}) collective-permute-start(bf16[128,1024]{1,0:T(8,128)(2,1)S(1)} %fusion.63), channel_id=1, source_target_pairs={{448,0},{0,64},{64,128},{128,192},{192,256},{256,320},{320,384},{3... | collective-permute-start | bytes 786440 | tf_op jit(solution)/shard_map/ppermute | solution.py:18
  130.8 18.6 %copy-start.2 = (bf16[128,1024]{1,0:T(8,128)(2,1)}, bf16[128,1024]{1,0:T(8,128)(2,1)S(1)}, u32[]{:S(2)}) copy-start(bf16[128,1024]{1,0:T(8,128)(2,1)S(1)} %collective-permute-done) | copy-start | bytes 786436
  131.0 0.6 copy-start.21
  131.3 4.4 copy-start.5
  131.6 0.9 copy-start.17
  132.3 152.3 %reduce-scatter.3.cloned.1.call-start = ((), (), s32[]{:S(2)}) async-start(), calls=%async_computation.4 | async-start | bytes 1114112 | tf_op jit(solution)/shard_map/reduce_scatter | solution.py:128
  148.8 212.1 %reduce-scatter.5.cloned.1.call-start = ((), (), s32[]{:S(2)}) async-start(), calls=%async_computation.5 | async-start | bytes 1114112 | tf_op jit(solution)/shard_map/reduce_scatter | solution.py:128
  210.3 2.6 copy-start.9
  210.3 2.6 copy-start.11
  218.1 3.2 copy-start.10
  218.1 3.2 copy-start.12
  221.3 2.6 copy-start.9
  221.3 2.6 copy-start.11
  229.1 3.1 copy-start.10
  229.1 3.1 copy-start.12
  232.3 3.8 copy-start.4
  232.3 6.1 %copy-start.7 = (bf16[2048,256]{1,0:T(8,128)(2,1)S(1)}, bf16[2048,256]{1,0:T(8,128)(2,1)}, u32[]{:S(2)}) copy-start(bf16[2048,256]{1,0:T(8,128)(2,1)} %all-gather.5.cloned.1.call-done) | copy-start | bytes 3145732
  242.3 44.9 %copy-start.20 = (f32[128]{0:T(128)S(1)}, f32[128]{0:T(128)}, u32[]{:S(2)}) copy-start(f32[128]{0:T(128)} %copy-done.19) | copy-start | bytes 1540
  246.3 114.7 %copy-start.6 = (f32[128,256]{1,0:T(8,128)S(1)}, f32[128,256]{1,0:T(8,128)}, u32[]{:S(2)}) copy-start(f32[128,256]{1,0:T(8,128)} %copy-done.5) | copy-start | bytes 393220
  246.3 114.7 %copy-start.18 = (f32[128]{0:T(128)S(1)}, f32[128]{0:T(128)}, u32[]{:S(2)}) copy-start(f32[128]{0:T(128)} %copy-done.17) | copy-start | bytes 1540
  246.3 117.3 %copy-start.3 = (bf16[128,1024]{1,0:T(8,128)(2,1)S(1)}, bf16[128,1024]{1,0:T(8,128)(2,1)}, u32[]{:S(2)}) copy-start(bf16[128,1024]{1,0:T(8,128)(2,1)} %copy-done.2) | copy-start | bytes 786436
  246.3 117.3 %copy-start.22 = (f32[128]{0:T(128)S(1)}, f32[128]{0:T(128)}, u32[]{:S(2)}) copy-start(f32[128]{0:T(128)} %copy-done.21) | copy-start | bytes 1540
  248.5 183.0 %all-reduce.3.cloned.1.call-start = ((), (), s32[]{:S(2)}) async-start(), calls=%async_computation.6 | async-start | bytes 4194304 | tf_op jit(solution)/shard_map/psum | solution.py:11
  365.6 228.4 %all-reduce.5.cloned.1.call-start = ((), (), s32[]{:S(2)}) async-start(), calls=%async_computation.7 | async-start | bytes 4194304 | tf_op jit(solution)/shard_map/psum | solution.py:12
  434.5 10.8 %collective-permute-start.1 = (bf16[128,1024]{1,0:T(8,128)(2,1)S(1)}, bf16[128,1024]{1,0:T(8,128)(2,1)S(1)}, u32[]{:S(2)}, u32[]{:S(2)}) collective-permute-start(bf16[128,1024]{1,0:T(8,128)(2,1)S(1)} %add_convert_fusion), channel_id=1, source_target_pairs={{448,0},{0,64},{64,128},{128,192},{192,256},{256,320},{320,384},{3... | collective-permute-start | bytes 786440 | tf_op jit(solution)/shard_map/ppermute | solution.py:18
Sparse Core Ops, SparseCore 0:
  12.8 77.9 all-gather.2
  132.5 73.2 all-gather.4
  208.5 76.0 reduce-scatter.2
  288.1 72.8 reduce-scatter.4
  365.8 65.7 all-reduce.2
  434.6 159.3 all-reduce.4
